TPU v7x, 256 devices: a whole 4x4x8 slice. The times are simulated.
256 devices in a mesh: dp: 16 (over y, x_lo, core), tensor: 16 (over x_hi, z).
Axes of the slice: x: 4 (x_hi: 2, x_lo: 2; x = x_hi * 2 + x_lo), y: 4, z: 8, core: 2. Of those that a mesh axis runs over, the one named last changes fastest.
Arguments:
- gate_pre: bfloat16 [28, 512, 16384], P(None, 'tensor', 'dp'), parts along dimension 2, may hold values from -6 to 6
- up_pre: bfloat16 [28, 512, 16384], P(None, 'tensor', 'dp'), parts along dimension 2, may hold values from -6 to 6
- down_weight: bfloat16 [28, 512, 4096], P(None, 'tensor'), may hold values from -0.0625 to 0.0625
Outputs:
- mixed: bfloat16 [4096, 16384], P('tensor', 'dp'), parts along dimension 1
There are 16 independent parts, one for each index of `dp`. A program takes and returns all parts, laid end to end along the dimension named above; an argument that names none is the same for every part. Nothing has to cross between parts.
All inputs are finite; a program needn't handle non-finite values.
Results may differ from a plain program's by a relative error of at most 0.024.
Values may be sent and summed in bfloat16 or wider, within the bound.
A program may use at most 128 MiB of HBM per device.

v0:
```python
import math

import jax
import jax.numpy as jnp
import numpy as np
from jax import lax
from jax.sharding import PartitionSpec as P


def partner_2(value, axis, distance):
    mask = 2**distance
    pairs = [(source, source ^ mask) for source in range(lax.axis_size(axis))]
    return lax.ppermute(value, axis, pairs)


def character(value, prime_order):
    residue = value % prime_order
    if residue == 0:
        return 0
    squares_list = [index * index % prime_order for index in range(1, prime_order)]
    return 1 if residue in squares_list else -1


def paley_matrix():
    prime_order = 13
    conference = np.zeros((14, 14))
    conference[0, 1:] = 1.0
    conference[1:, 0] = 1.0
    for row_index in range(prime_order):
        for col_index in range(prime_order):
            conference[row_index + 1, col_index + 1] = character(col_index - row_index, prime_order)
    first = np.array([[1.0, 1.0], [1.0, -1.0]])
    second = np.array([[1.0, -1.0], [-1.0, -1.0]])
    return np.kron(conference, first) + np.kron(np.eye(14), second)


def sylvester(order):
    matrix = np.ones((1, 1))
    basic = np.array([[1.0, 1.0], [1.0, -1.0]])
    while matrix.shape[0] < order:
        matrix = np.kron(basic, matrix)
    return matrix


def both_factors(values, left_factor, right_factor):
    values = jnp.einsum(
        "ij,jbt->ibt", left_factor, values.astype(jnp.float32), precision=lax.Precision.DEFAULT
    )
    return jnp.einsum("bc,act->abt", right_factor, values, precision=lax.Precision.HIGH)


def body(gate_pre, up_pre, down_weight):
    hidden = (jax.nn.silu(gate_pre.astype(jnp.float32)) * up_pre.astype(jnp.float32)).astype(
        jnp.bfloat16
    )
    devices = lax.axis_size("tensor")
    left_factor = jnp.asarray(paley_matrix(), jnp.float32)
    local_width = hidden.shape[1]
    inner_factor = jnp.asarray(sylvester(local_width), jnp.float32)
    current = both_factors(hidden, left_factor, inner_factor)
    position = lax.axis_index("tensor")
    for bit_level in range(devices.bit_length() - 1):
        partner = partner_2(current.astype(jnp.bfloat16), "tensor", bit_level).astype(current.dtype)
        parity = position // 2**bit_level % 2
        flip_sign = (1 - 2 * parity).astype(jnp.float32)
        current = partner + flip_sign * current
    rotated = (current * (1.0 / math.sqrt(hidden.shape[0] * devices * local_width))).astype(
        jnp.bfloat16
    )
    return lax.psum_scatter(
        lax.dot_general(
            down_weight, rotated, (((0, 1), (0, 1)), ((), ())), preferred_element_type=jnp.float32
        ).astype(jnp.bfloat16),
        "tensor",
        scatter_dimension=0,
        tiled=True,
    )


def solution(mesh):
    in_specs = (P(None, "tensor", "dp"), P(None, "tensor", "dp"), P(None, "tensor", None))
    out_specs = P("tensor", "dp")
    return jax.shard_map(body, mesh=mesh, in_specs=in_specs, out_specs=out_specs, check_vma=False)
```

profile of v0, /device:TPU:32, one launch (start us, length us, event | category | flops | bytes accessed | tf_op | source)
XLA Modules:
  0.0 536.8 jit_solution(2434385821058037137)
XLA Ops:
  6.5 0.0 reduce-scatter.2.cloned.1.call-start
  6.5 3.2 fusion.7
  9.8 0.0 copy-done.2
  9.8 0.0 copy-start.1
  9.8 2.5 fusion.9
  12.2 0.0 copy-done.1
  12.2 4.3 fusion.5
  16.6 1.8 copy-done
  18.4 1.5 convert_bitcast_fusion
  19.9 1.8 collective-permute-start
  21.8 40.1 %collective-permute-done = bf16[28,32,1024]{2,1,0:T(8,128)(2,1)S(1)} collective-permute-done((bf16[28,32,1024]{2,1,0:T(8,128)(2,1)}, bf16[28,32,1024]{2,1,0:T(8,128)(2,1)S(1)}, u32[]{:S(2)}, u32[]{:S(2)}) %collective-permute-start) | collective-permute-done | bytes 1835040 | tf_op jit(solution)/shard_map/ppermute | solution.py:13
  61.9 4.0 fusion.15
  65.8 3.3 collective-permute-start.1
  69.1 78.0 %collective-permute-done.1 = bf16[28,32,1024]{2,1,0:T(8,128)(2,1)} collective-permute-done((bf16[28,32,1024]{2,1,0:T(8,128)(2,1)}, bf16[28,32,1024]{2,1,0:T(8,128)(2,1)}, u32[]{:S(2)}, u32[]{:S(2)}) %collective-permute-start.1) | collective-permute-done | bytes 1835040 | tf_op jit(solution)/shard_map/ppermute | solution.py:13
  147.1 4.9 fusion.8
  152.0 4.6 collective-permute-start.2
  156.6 51.7 %collective-permute-done.2 = bf16[28,32,1024]{2,1,0:T(8,128)(2,1)} collective-permute-done((bf16[28,32,1024]{2,1,0:T(8,128)(2,1)}, bf16[28,32,1024]{2,1,0:T(8,128)(2,1)}, u32[]{:S(2)}, u32[]{:S(2)}) %collective-permute-start.2) | collective-permute-done | bytes 1835040 | tf_op jit(solution)/shard_map/ppermute | solution.py:13
  208.3 6.0 %fusion.13 = bf16[28,32,1024]{2,1,0:T(8,128)(2,1)} fusion(f32[]{:T(128)S(6)} %convert_element_type.67, bf16[28,32,1024]{2,1,0:T(8,128)(2,1)} %collective-permute-done.1, f32[]{:T(128)S(6)} %convert_element_type.70, bf16[28,32,1024]{2,1,0:T(8,128)(2,1)} %collective-permute-done.2, f32[28,1024,32]{1,2,0:T(8,128)} %copy-done, f32[]{:T(128)S(6)} %convert_element_type.64, ...), kind=kLoop, calls=%fused_computation.21 | loop fusion | flops 9175040 | bytes 11010060 | tf_op jit(solution)/shard_map/convert_element_type | solution.py:63
  214.2 3.1 collective-permute-start.3
  217.3 39.5 %collective-permute-done.3 = bf16[28,32,1024]{2,1,0:T(8,128)(2,1)} collective-permute-done((bf16[28,32,1024]{2,1,0:T(8,128)(2,1)}, bf16[28,32,1024]{2,1,0:T(8,128)(2,1)}, u32[]{:S(2)}, u32[]{:S(2)}) %collective-permute-start.3) | collective-permute-done | bytes 1835040 | tf_op jit(solution)/shard_map/ppermute | solution.py:13
  256.8 18.5 %fusion = bf16[4096,1024]{0,1:T(8,128)(2,1)} fusion(bf16[28,32,4096]{2,1,0:T(8,128)(2,1)} %param.7, bf16[28,32,1024]{2,1,0:T(8,128)(2,1)} %collective-permute-done.3, f32[]{:T(128)S(6)} %convert_element_type.73, bf16[28,32,1024]{2,1,0:T(8,128)(2,1)} %collective-permute-done.2, bf16[28,32,1024]{2,1,0:T(8,128)(2,1)} %collective-permute-done.1, ...), kind=kOutput, calls=%fused_computation.1 | convolution fusion | flops 7533232128 | bytes 26738704 | tf_op jit(solution)/shard_map/dot_general | solution.py:71
  275.3 0.0 reduce-scatter.2.cloned.1.call-update
  275.3 252.6 %reduce-scatter.2.cloned.1.call-done = bf16[256,1024]{0,1:T(8,128)(2,1)} async-done(((bf16[4096,1024]{0,1:T(8,128)(2,1)}), bf16[256,1024]{0,1:T(8,128)(2,1)}) %reduce-scatter.2.cloned.1.call-update) | async-done | bytes 524304 | tf_op jit(solution)/shard_map/reduce_scatter | solution.py:70
  527.9 2.0 copy.6
  (2 shorter events, 0.0 us)
Async XLA Ops:
  6.5 3.2 copy-start.2
  6.5 521.4 %reduce-scatter.2.cloned.1.call-start = ((), (), s32[]{:S(2)}) async-start(), calls=%async_computation.1 | async-start | bytes 8912896 | tf_op jit(solution)/shard_map/reduce_scatter | solution.py:70
  9.8 2.5 copy-start.1
  16.6 1.8 copy-start
  19.9 42.0 %collective-permute-start = (bf16[28,32,1024]{2,1,0:T(8,128)(2,1)}, bf16[28,32,1024]{2,1,0:T(8,128)(2,1)S(1)}, u32[]{:S(2)}, u32[]{:S(2)}) collective-permute-start(bf16[28,32,1024]{2,1,0:T(8,128)(2,1)} %convert_bitcast_fusion), channel_id=1, source_target_pairs={{0,1},{1,0},{2,3},{3,2},{4,5},{5,4},{6,7},{7,6},{8,9},{9,8},{10,11... | collective-permute-start | bytes 5505032 | tf_op jit(solution)/shard_map/ppermute | solution.py:13
  65.8 81.2 %collective-permute-start.1 = (bf16[28,32,1024]{2,1,0:T(8,128)(2,1)}, bf16[28,32,1024]{2,1,0:T(8,128)(2,1)}, u32[]{:S(2)}, u32[]{:S(2)}) collective-permute-start(bf16[28,32,1024]{2,1,0:T(8,128)(2,1)} %fusion.15), channel_id=1, source_target_pairs={{0,2},{1,3},{2,0},{3,1},{4,6},{5,7},{6,4},{7,5},{8,10},{9,11},{10,... | collective-permute-start | bytes 5505032 | tf_op jit(solution)/shard_map/ppermute | solution.py:13
  152.0 56.3 %collective-permute-start.2 = (bf16[28,32,1024]{2,1,0:T(8,128)(2,1)}, bf16[28,32,1024]{2,1,0:T(8,128)(2,1)}, u32[]{:S(2)}, u32[]{:S(2)}) collective-permute-start(bf16[28,32,1024]{2,1,0:T(8,128)(2,1)} %fusion.8), channel_id=1, source_target_pairs={{0,4},{1,5},{2,6},{3,7},{4,0},{5,1},{6,2},{7,3},{8,12},{9,13},{10,... | collective-permute-start | bytes 5505032 | tf_op jit(solution)/shard_map/ppermute | solution.py:13
  214.2 42.6 %collective-permute-start.3 = (bf16[28,32,1024]{2,1,0:T(8,128)(2,1)}, bf16[28,32,1024]{2,1,0:T(8,128)(2,1)}, u32[]{:S(2)}, u32[]{:S(2)}) collective-permute-start(bf16[28,32,1024]{2,1,0:T(8,128)(2,1)} %fusion.13), channel_id=1, source_target_pairs={{0,8},{1,9},{2,10},{3,11},{4,12},{5,13},{6,14},{7,15},{8,0},{9,1},... | collective-permute-start | bytes 5505032 | tf_op jit(solution)/shard_map/ppermute | solution.py:13
Sparse Core Ops, SparseCore 0:
  275.4 252.4 reduce-scatter.1
where the time goes:
time: 538 us; the launch traced here: 537 us
  waiting for transfers between devices  462 us (86%)
  matrix products  25.3 us (5%)
  other arithmetic  19.6 us (4%)
  between operations  13.4 us (2%)
  starting transfers between devices  12.8 us (2%)
    reduce_scatter x1, waiting for transfers between devices, body(): lax.psum_scatter(lax.dot_general(down_weight, rotated, (((0, 1), (0, 1)),...  253 us
    ppermute x4, waiting for transfers between devices, partner_2(): return lax.ppermute(value, axis, pairs)  209 us
    dot_general x1, matrix products, body(): lax.dot_general(down_weight, rotated, (((0, 1), (0, 1)), ((), ())), prefe...  18.5 us
    convert_element_type x4, other arithmetic, body(): current.astype(jnp.bfloat16)  16.4 us
    ppermute x4, starting transfers between devices, partner_2(): return lax.ppermute(value, axis, pairs)  12.8 us
  transfers between devices with their start and end apart: 5, of which 5 were waited for; matrix products, arithmetic and copies ran while one was open for 0% of the time, Pallas kernels for 0%

commit v1 on v0

v1 whole, which is shorter than its diff:
```python
import functools
import math

import jax
import jax.numpy as jnp
import numpy as np
from jax import lax
from jax.experimental import pallas as pl
from jax.experimental.pallas import tpu as pltpu
from jax.sharding import PartitionSpec as P

MESH = pl.DeviceIdType.MESH
BF = jnp.bfloat16
F32 = jnp.float32

NZ = 8
KL = 896
KB = 112
TOKENS = 1024
TH = 512
TQ = 256
CW = 128


def character(value, prime_order):
    residue = value % prime_order
    if residue == 0:
        return 0
    squares_list = [index * index % prime_order for index in range(1, prime_order)]
    return 1 if residue in squares_list else -1


def paley_matrix():
    prime_order = 13
    conference = np.zeros((14, 14))
    conference[0, 1:] = 1.0
    conference[1:, 0] = 1.0
    for row_index in range(prime_order):
        for col_index in range(prime_order):
            conference[row_index + 1, col_index + 1] = character(col_index - row_index, prime_order)
    first = np.array([[1.0, 1.0], [1.0, -1.0]])
    second = np.array([[1.0, -1.0], [-1.0, -1.0]])
    return np.kron(conference, first) + np.kron(np.eye(14), second)


def sylvester(order):
    matrix = np.ones((1, 1))
    basic = np.array([[1.0, 1.0], [1.0, -1.0]])
    while matrix.shape[0] < order:
        matrix = np.kron(basic, matrix)
    return matrix


def place(d):
    d %= NZ
    return max(0, 2 * (4 - d) - 1) if d <= 4 else 2 * (d - 4)


GROUPS = ((0, 3), (3, 2), (5, 3))
NG = len(GROUPS)
CHAINS = (("a+", 0, 1, 4), ("b-", 1, -1, 4), ("b+", 1, 1, 3), ("a-", 0, -1, 3))


def kernel(scale, gate, up, weight, hmat, out,
           gbuf, ubuf, hbuf, hid, rot, rec1, snd2, stg, wbuf, part, rsend, rrecv,
           load_sem, p1s, p1r, p2s, p2r, xs, xr, ys, yr, cs, cr, hs, hr, rs, rr):
    dp = lax.axis_index("dp")
    tn = lax.axis_index("tensor")
    y = dp // 4
    xl = lax.rem(dp // 2, 2)
    core = lax.rem(dp, 2)
    xh = tn // NZ
    z = lax.rem(tn, NZ)
    block = y * 2 + xl
    crossed = core != xh

    def dev(y_=None, xl_=None, core_=None, xh_=None, z_=None):
        y_ = y if y_ is None else y_
        xl_ = xl if xl_ is None else xl_
        core_ = core if core_ is None else core_
        xh_ = xh if xh_ is None else xh_
        z_ = z if z_ is None else z_
        return (y_ * 4 + xl_ * 2 + core_, xh_ * NZ + z_)

    def zat(o):
        return lax.rem(z + (o % NZ), NZ)

    def yat(o):
        return lax.rem(y + (o % 4), 4)

    def remote(src, dst, s, r, to):
        return pltpu.make_async_remote_copy(
            src_ref=src, dst_ref=dst, send_sem=s, recv_sem=r, device_id=to, device_id_type=MESH)

    sent = []

    def send(src, dst, s, r, to):
        c = remote(src, dst, s, r, to)
        c.start()
        sent.append(c)

    def recv(dst, s, r, frm):
        remote(dst, dst, s, r, frm).wait_recv()

    loads = []
    for t in range(2):
        ts = pl.ds(t * TH, TH)
        for i, (src, dst) in enumerate(((gate, gbuf), (up, ubuf))):
            c = pltpu.make_async_copy(src.at[:, ts], dst.at[:, ts], load_sem.at[t * 2 + i])
            c.start()
            loads.append(c)
    c = pltpu.make_async_copy(hmat, hbuf, load_sem.at[4])
    c.start()
    loads.append(c)

    barrier = pltpu.get_barrier_semaphore()
    partners = [dev(z_=zat(o)) for o in range(1, NZ)]
    partners += [dev(y_=yat(1)), dev(y_=yat(-1)), dev(core_=1 - core), dev(xh_=1 - xh)]
    partners += [dev(xl_=1 - xl, core_=xh, xh_=core)]
    for to in partners:
        pl.semaphore_signal(barrier, inc=1, device_id=to, device_id_type=MESH)

    @pl.when(crossed)
    def _():
        pl.semaphore_signal(barrier, inc=1, device_id=dev(core_=xh, xh_=core), device_id_type=MESH)
        pl.semaphore_wait(barrier, len(partners) + 1)

    @pl.when(jnp.logical_not(crossed))
    def _():
        pl.semaphore_wait(barrier, len(partners))

    rows1 = pl.ds(pl.multiple_of(block * KB, 16), KB)

    def cols1(j, zz):
        return pl.ds(pl.multiple_of(core * (NZ * 2 * CW) + zz * (2 * CW) + j * CW, 128), CW)

    def p1_send(j):
        for o in range(1, NZ):
            zz = zat(o)
            send(weight.at[rows1, cols1(j, zz)], rec1.at[j, z], p1s.at[j, o], p1r.at[j, o], dev(z_=zz))
        pltpu.make_async_copy(weight.at[rows1, cols1(j, z)], rec1.at[j, z], p1r.at[j, 0]).start()

    def p1_wait_rotate(j):
        pltpu.make_async_copy(weight.at[rows1, cols1(j, z)], rec1.at[j, z], p1r.at[j, 0]).wait()
        for o in range(1, NZ):
            zz = zat(-o)
            recv(rec1.at[j, zz], p1s.at[j, o], p1r.at[j, o], dev(z_=zz))
        v = [rec1[j, i].astype(F32) for i in range(NZ)]
        for bit in (1, 2, 4):
            v = [v[i] + v[i ^ bit] if not i & bit else v[i ^ bit] - v[i] for i in range(NZ)]
        for i in range(NZ):
            snd2[j, i] = v[i].astype(BF)

    def p2_send(j):
        for o in range(1, NZ):
            zz = zat(o)
            send(snd2.at[j, zz], stg.at[j, :, pl.ds(place(-o) * CW, CW)], p2s.at[j, o], p2r.at[j, o], dev(z_=zz))
        stg[j, :, pl.ds(place(0) * CW, CW)] = snd2[j, z]

    def gcols(g):
        return pl.ds(GROUPS[g][0] * CW, GROUPS[g][1] * CW)

    def wrows(s, b, n):
        return pl.ds(pl.multiple_of(s * KL + b * KB, 16), n)

    def x_copy(j, g, dst_xl, i):
        return remote(stg.at[j, :, gcols(g)], wbuf.at[j, wrows(xh, block, KB), gcols(g)],
                      xs.at[j, g, i], xr.at[j, g, i], dev(xl_=dst_xl, core_=xh, xh_=core))

    def p2_wait(j):
        for o in range(1, NZ):
            recv(stg.at[j, :, pl.ds(place(-o) * CW, CW)], p2s.at[j, o], p2r.at[j, o], dev(z_=zat(-o)))

    def x_send(j, g):
        c = x_copy(j, g, 1 - xl, 1)
        c.start()
        sent.append(c)

        @pl.when(crossed)
        def _():
            x_copy(j, g, xl, 0).start()

        @pl.when(jnp.logical_not(crossed))
        def _():
            pltpu.make_async_copy(stg.at[j, :, gcols(g)], wbuf.at[j, wrows(xh, block, KB), gcols(g)],
                                  xr.at[j, g, 0]).start()

    def x_finish(j, g):
        @pl.when(crossed)
        def _():
            x_copy(j, g, xl, 0).wait_send()

    def wblock(j, g, s, yy, n=2 * KB, off=0):
        return wbuf.at[j, wrows(s, yy * 2 + off, n), gcols(g)]

    def core_fwd(j, g, yy, i):
        ref = wblock(j, g, core, yy)
        send(ref, ref, cs.at[j, g, i], cr.at[j, g, i], dev(core_=1 - core))

    def y_own(j, g):
        own = wbuf.at[j, wrows(core, block, KB), gcols(g)]
        recv(own, xs.at[j, g, 0], xr.at[j, g, 0], dev(core_=xh, xh_=core))
        other = wbuf.at[j, wrows(core, y * 2 + 1 - xl, KB), gcols(g)]
        recv(other, xs.at[j, g, 1], xr.at[j, g, 1], dev(xl_=1 - xl, core_=xh, xh_=core))
        ref = wblock(j, g, core, y)
        send(ref, ref, ys.at[j, g, 0], yr.at[j, g, 0], dev(y_=yat(1)))
        send(ref, ref, ys.at[j, g, 1], yr.at[j, g, 1], dev(y_=yat(-1)))
        core_fwd(j, g, y, 0)

    def y_near(j, g):
        for i, step in ((0, 1), (1, -1)):
            frm = yat(-step)
            recv(wblock(j, g, core, frm), ys.at[j, g, i], yr.at[j, g, i], dev(y_=frm))
            half = wblock(j, g, core, frm, KB, i)
            send(half, half, ys.at[j, g, 2 + i], yr.at[j, g, 2 + i], dev(y_=yat(step)))
            core_fwd(j, g, frm, 1 + i)

    def y_far(j, g):
        far = yat(2)
        for i, step in ((0, 1), (1, -1)):
            recv(wblock(j, g, core, far, KB, i), ys.at[j, g, 2 + i], yr.at[j, g, 2 + i], dev(y_=yat(-step)))
        core_fwd(j, g, far, 3)

    def c_wait(j, g):
        for i, o in enumerate((0, -1, 1, 2)):
            recv(wblock(j, g, 1 - core, yat(o)), cs.at[j, g, i], cr.at[j, g, i], dev(core_=1 - core))

    def silu(t):
        loads[2 * t].wait()
        loads[2 * t + 1].wait()

        def step(i, carry):
            rows = pl.ds(pl.multiple_of(i * 128, 128), 128)
            cols = pl.ds(t * TH, TH)
            half = gbuf[rows, cols].astype(F32) * 0.5
            value = (half + half * jnp.tanh(half)) * ubuf[rows, cols].astype(F32)
            hid[xh, cols, rows] = value.astype(BF).T
            return carry

        lax.fori_loop(0, KL // 128, step, 0)

    def h_ref(t, s):
        return hid.at[s, pl.ds(t * TH, TH)]

    def h_send(t):
        send(h_ref(t, xh), h_ref(t, xh), hs.at[t], hr.at[t], dev(xh_=1 - xh))

    def rotate(t):
        if t == 0:
            loads[4].wait()
        recv(h_ref(t, 1 - xh), hs.at[t], hr.at[t], dev(xh_=1 - xh))
        rows = pl.ds(t * TH, TH)
        for n0, n in ((0, 256), (256, 256), (512, 256), (768, 128)):
            m = hbuf[:, n0:n0 + n]
            l0 = jnp.dot(hid[0, rows], m, preferred_element_type=F32)
            l1 = jnp.dot(hid[1, rows], m, preferred_element_type=F32)
            rot[rows, n0:n0 + n] = ((l0 + l1) * scale).astype(BF)
            rot[rows, KL + n0:KL + n0 + n] = ((l0 - l1) * scale).astype(BF)

    def partial(p, j, t, g):
        first, n = GROUPS[g]
        for i in range(0, n, 2):
            w = min(2, n - i) * CW
            c0 = (first + i) * CW
            part[p % 2, :, c0:c0 + w] = jnp.dot(
                rot[pl.ds(t * TH, TH)], wbuf[j, :, c0:c0 + w], preferred_element_type=F32)

    def own_part(p, half, m):
        c0 = place(m) * CW
        return part[p % 2, half * TQ:(half + 1) * TQ, c0:c0 + CW]

    def rs_wait(p, k, m):
        _, half, d, _ = CHAINS[k]
        recv(rrecv.at[p, k, m], rs.at[p, k, m], rr.at[p, k, m], dev(z_=zat(-d)))
        return rrecv[p, k, m].astype(F32)

    def rs_hop(p, k, m):
        _, half, d, first = CHAINS[k]
        value = own_part(p, half, d * m)
        if m < first:
            value = value + rs_wait(p, k, m)
        rsend[p, k, m - 1] = value.astype(BF)
        send(rsend.at[p, k, m - 1], rrecv.at[p, k, m - 1], rs.at[p, k, m - 1], rr.at[p, k, m - 1],
             dev(z_=zat(d)))

    def rs_step(p, s):
        for k in range(4):
            m = CHAINS[k][3] - s
            if m >= 1:
                rs_hop(p, k, m)

    def rs_final(p, j, t):
        for half, (ka, kb) in ((0, (3, 0)), (1, (2, 1))):
            value = own_part(p, half, 0) + rs_wait(p, ka, 0) + rs_wait(p, kb, 0)
            c0 = t * TH + half * TQ
            out[j * CW:(j + 1) * CW, c0:c0 + TQ] = value.T.astype(BF)

    p1_send(0)
    p1_send(1)
    silu(0)
    h_send(0)
    p1_wait_rotate(0)
    p2_send(0)
    silu(1)
    p1_wait_rotate(1)
    p2_send(1)
    p2_wait(0)
    for g in range(NG):
        x_send(0, g)
    h_send(1)
    for g in range(NG):
        y_own(0, g)
    y_near(0, 0)
    p2_wait(1)
    for g in range(NG):
        x_send(1, g)
    y_far(0, 0)
    y_near(0, 1)
    rotate(0)
    c_wait(0, 0)
    partial(0, 0, 0, 0)
    rs_step(0, 0)
    y_far(0, 1)
    y_near(0, 2)
    for g in range(NG):
        y_own(1, g)
    c_wait(0, 1)
    partial(0, 0, 0, 1)
    rs_step(0, 1)
    y_far(0, 2)
    c_wait(0, 2)
    partial(0, 0, 0, 2)
    rs_step(0, 2)
    y_near(1, 0)
    rs_step(0, 3)
    y_far(1, 0)
    rotate(1)
    for g in range(NG):
        partial(1, 0, 1, g)
    rs_step(1, 0)
    y_near(1, 1)
    rs_final(0, 0, 0)
    rs_step(1, 1)
    y_far(1, 1)
    y_near(1, 2)
    c_wait(1, 0)
    partial(2, 1, 0, 0)
    rs_step(2, 0)
    rs_step(1, 2)
    y_far(1, 2)
    c_wait(1, 1)
    partial(2, 1, 0, 1)
    rs_step(1, 3)
    rs_step(2, 1)
    c_wait(1, 2)
    partial(2, 1, 0, 2)
    rs_final(1, 0, 1)
    rs_step(2, 2)
    for g in range(NG):
        partial(3, 1, 1, g)
    rs_step(3, 0)
    rs_step(2, 3)
    rs_step(3, 1)
    rs_final(2, 1, 0)
    rs_step(3, 2)
    rs_step(3, 3)
    rs_final(3, 1, 1)

    for c in sent:
        c.wait_send()
    for j in range(2):
        for g in range(NG):
            x_finish(j, g)


def body(gate_pre, up_pre, down_weight):
    hmat = jnp.asarray(np.kron(paley_matrix(), sylvester(32)), BF)
    dma = pltpu.SemaphoreType.DMA
    any_spec = pl.BlockSpec(memory_space=pl.ANY)
    return pl.pallas_call(
        functools.partial(kernel, 1.0 / math.sqrt(16 * KL)),
        out_shape=jax.ShapeDtypeStruct((2 * CW, TOKENS), BF),
        in_specs=[any_spec] * 4,
        out_specs=pl.BlockSpec(memory_space=pltpu.VMEM),
        scratch_shapes=[
            pltpu.VMEM((KL, TOKENS), BF),
            pltpu.VMEM((KL, TOKENS), BF),
            pltpu.VMEM((KL, KL), BF),
            pltpu.VMEM((2, TOKENS, KL), BF),
            pltpu.VMEM((TOKENS, 2 * KL), BF),
            pltpu.VMEM((2, NZ, KB, CW), BF),
            pltpu.VMEM((2, NZ, KB, CW), BF),
            pltpu.VMEM((2, KB, NZ * CW), BF),
            pltpu.VMEM((2, 2 * KL, NZ * CW), BF),
            pltpu.VMEM((2, TH, NZ * CW), F32),
            pltpu.VMEM((4, 4, 4, TQ, CW), BF),
            pltpu.VMEM((4, 4, 4, TQ, CW), BF),
            dma((5,)),
            dma((2, NZ)), dma((2, NZ)),
            dma((2, NZ)), dma((2, NZ)),
            dma((2, NG, 2)), dma((2, NG, 2)),
            dma((2, NG, 4)), dma((2, NG, 4)),
            dma((2, NG, 4)), dma((2, NG, 4)),
            dma((2,)), dma((2,)),
            dma((4, 4, 4)), dma((4, 4, 4)),
        ],
        compiler_params=pltpu.CompilerParams(
            collective_id=0, has_side_effects=True, vmem_limit_bytes=56 << 20),
        name="rotated_down_projection",
    )(gate_pre.reshape(KL, TOKENS), up_pre.reshape(KL, TOKENS),
      down_weight.reshape(KL, 16 * 2 * CW), hmat)


def solution(mesh):
    in_specs = (P(None, "tensor", "dp"), P(None, "tensor", "dp"), P(None, "tensor", None))
    out_specs = P("tensor", "dp")
    return jax.shard_map(body, mesh=mesh, in_specs=in_specs, out_specs=out_specs, check_vma=False)
```

time: 538 us -> 126 us (0.23)
  waiting for transfers between devices: 462 us -> 0 us
  Pallas kernels: 0 us -> 123 us
  matrix products: 25.3 us -> 0 us
  other arithmetic: 19.6 us -> 0 us
  between operations: 13.4 us -> 0.01 us
  starting transfers between devices: 12.8 us -> 0 us
    reduce_scatter x1 -> x0, waiting for transfers between devices: 253 us -> none  [body(): lax.psum_scatter(lax.dot_general(down_weight, rotated, (((0, 1), (0, 1)),...]
    ppermute x4 -> x0, waiting for transfers between devices: 209 us -> none  [partner_2(): return lax.ppermute(value, axis, pairs)]
    pallas_call x0 -> x1, Pallas kernels: none -> 123 us  [body(): pl.pallas_call(functools.partial(kernel, 1.0 / math.sqrt(16 * KL)), out_s...]
    dot_general x3 -> x0, matrix products: 25.3 us -> none  [the longest x1 18.5 us: body(): lax.dot_general(down_weight, rotated, (((0, 1), (0, 1)), ((), ())), prefe...]
    convert_element_type x5 -> x0, other arithmetic: 19.6 us -> none  [the longest x4 16.4 us: body(): current.astype(jnp.bfloat16)]
    ppermute x4 -> x0, starting transfers between devices: 12.8 us -> none  [partner_2(): return lax.ppermute(value, axis, pairs)]
  transfers between devices with their start and end apart: 5 -> 0, of which waited for: 5 -> 0; matrix products, arithmetic and copies ran while one was open for 0% -> 0% of each run, Pallas kernels for 0% -> 0%
where the time goes in v1:
time: 126 us; the launch traced here: 125 us
  Pallas kernels  123 us (98%)
  local copies, waits for them, and re-layouts  1.87 us (1%)
    pallas_call x1, Pallas kernels, body(): pl.pallas_call(functools.partial(kernel, 1.0 / math.sqrt(16 * KL)), out_s...  123 us

profile of v1, /device:TPU:32, one launch (start us, length us, event | category | flops | bytes accessed | tf_op | source)
XLA Modules:
  0.0 125.4 jit_solution(11961057357149109243)
XLA Ops:
  0.0 123.5 %rotated_down_projection.1 = bf16[256,1024]{1,0:T(8,128)(2,1)} custom-call(bf16[896,1024]{1,0:T(8,128)(2,1)} %bitcast.4, bf16[896,1024]{1,0:T(8,128)(2,1)} %bitcast.5, bf16[896,4096]{1,0:T(8,128)(2,1)} %bitcast.3, bf16[896,896]{1,0:T(8,128)(2,1)} %constant.2.clone.hmat), custom_call_target="tpu_custom_call" | custom-call | tf_op jit(solution)/shard_map/rotated_down_projection/pallas_call | solution.py:380
  123.5 1.9 %copy.6 = bf16[256,1024]{1,0:T(8,128)(2,1)} copy(bf16[256,1024]{1,0:T(8,128)(2,1)} %rotated_down_projection.1) | data formatting | bytes 1048576

commit v2 on v1

--- a/solution.py
+++ b/solution.py
@@ -19,6 +19,8 @@
 TOKENS = 1024
 TH = 512
 TQ = 256
+NQ = TOKENS // TQ
+HX = 64
 CW = 128
 
 
@@ -56,9 +58,15 @@
     return max(0, 2 * (4 - d) - 1) if d <= 4 else 2 * (d - 4)
 
 
-GROUPS = ((0, 3), (3, 2), (5, 3))
+GROUPS = ((0, 1), (1, 2), (3, 2), (5, 3))
 NG = len(GROUPS)
-CHAINS = (("a+", 0, 1, 4), ("b-", 1, -1, 4), ("b+", 1, 1, 3), ("a-", 0, -1, 3))
+
+
+def chain(q, k):
+    return (1, 4 - q % 2) if k == 0 else (-1, 3 + q % 2)
+
+
+NAME = "rotated_down_projection"
 
 
 def kernel(scale, gate, up, weight, hmat, out,
@@ -103,15 +111,18 @@
         remote(dst, dst, s, r, frm).wait_recv()
 
     loads = []
-    for t in range(2):
-        ts = pl.ds(t * TH, TH)
-        for i, (src, dst) in enumerate(((gate, gbuf), (up, ubuf))):
-            c = pltpu.make_async_copy(src.at[:, ts], dst.at[:, ts], load_sem.at[t * 2 + i])
-            c.start()
-            loads.append(c)
-    c = pltpu.make_async_copy(hmat, hbuf, load_sem.at[4])
-    c.start()
-    loads.append(c)
+
+    def load(src, dst):
+        c = pltpu.make_async_copy(src, dst, load_sem.at[len(loads)])
+        c.start()
+        loads.append(c)
+
+    def load_all():
+        for t in range(2):
+            ts = pl.ds(t * TH, TH)
+            load(gate.at[:, ts], gbuf.at[:, ts])
+            load(up.at[:, ts], ubuf.at[:, ts])
+        load(hmat, hbuf)
 
     barrier = pltpu.get_barrier_semaphore()
     partners = [dev(z_=zat(o)) for o in range(1, NZ)]
@@ -123,11 +134,15 @@
     @pl.when(crossed)
     def _():
         pl.semaphore_signal(barrier, inc=1, device_id=dev(core_=xh, xh_=core), device_id_type=MESH)
-        pl.semaphore_wait(barrier, len(partners) + 1)
-
-    @pl.when(jnp.logical_not(crossed))
-    def _():
-        pl.semaphore_wait(barrier, len(partners))
+
+    def meet():
+        @pl.when(crossed)
+        def _():
+            pl.semaphore_wait(barrier, len(partners) + 1)
+
+        @pl.when(jnp.logical_not(crossed))
+        def _():
+            pl.semaphore_wait(barrier, len(partners))
 
     rows1 = pl.ds(pl.multiple_of(block * KB, 16), KB)
 
@@ -152,7 +167,7 @@
             snd2[j, i] = v[i].astype(BF)
 
     def p2_send(j):
-        for o in range(1, NZ):
+        for o in sorted(range(1, NZ), key=lambda o: place(-o)):
             zz = zat(o)
             send(snd2.at[j, zz], stg.at[j, :, pl.ds(place(-o) * CW, CW)], p2s.at[j, o], p2r.at[j, o], dev(z_=zz))
         stg[j, :, pl.ds(place(0) * CW, CW)] = snd2[j, z]
@@ -167,11 +182,13 @@
         return remote(stg.at[j, :, gcols(g)], wbuf.at[j, wrows(xh, block, KB), gcols(g)],
                       xs.at[j, g, i], xr.at[j, g, i], dev(xl_=dst_xl, core_=xh, xh_=core))
 
-    def p2_wait(j):
+    crossing = []
+
+    def x_send(j, g):
+        crossing.append((j, g))
         for o in range(1, NZ):
-            recv(stg.at[j, :, pl.ds(place(-o) * CW, CW)], p2s.at[j, o], p2r.at[j, o], dev(z_=zat(-o)))
-
-    def x_send(j, g):
+            if 0 <= place(-o) - GROUPS[g][0] < GROUPS[g][1]:
+                recv(stg.at[j, :, pl.ds(place(-o) * CW, CW)], p2s.at[j, o], p2r.at[j, o], dev(z_=zat(-o)))
         c = x_copy(j, g, 1 - xl, 1)
         c.start()
         sent.append(c)
@@ -207,13 +224,13 @@
         send(ref, ref, ys.at[j, g, 1], yr.at[j, g, 1], dev(y_=yat(-1)))
         core_fwd(j, g, y, 0)
 
-    def y_near(j, g):
-        for i, step in ((0, 1), (1, -1)):
-            frm = yat(-step)
-            recv(wblock(j, g, core, frm), ys.at[j, g, i], yr.at[j, g, i], dev(y_=frm))
-            half = wblock(j, g, core, frm, KB, i)
-            send(half, half, ys.at[j, g, 2 + i], yr.at[j, g, 2 + i], dev(y_=yat(step)))
-            core_fwd(j, g, frm, 1 + i)
+    def y_near(j, g, i):
+        step = 1 - 2 * i
+        frm = yat(-step)
+        recv(wblock(j, g, core, frm), ys.at[j, g, i], yr.at[j, g, i], dev(y_=frm))
+        half = wblock(j, g, core, frm, KB, i)
+        send(half, half, ys.at[j, g, 2 + i], yr.at[j, g, 2 + i], dev(y_=yat(step)))
+        core_fwd(j, g, frm, 1 + i)
 
     def y_far(j, g):
         far = yat(2)
@@ -221,7 +238,7 @@
             recv(wblock(j, g, core, far, KB, i), ys.at[j, g, 2 + i], yr.at[j, g, 2 + i], dev(y_=yat(-step)))
         core_fwd(j, g, far, 3)
 
-    def c_wait(j, g):
+    def w_wait(j, g):
         for i, o in enumerate((0, -1, 1, 2)):
             recv(wblock(j, g, 1 - core, yat(o)), cs.at[j, g, i], cr.at[j, g, i], dev(core_=1 - core))
 
@@ -239,17 +256,19 @@
 
         lax.fori_loop(0, KL // 128, step, 0)
 
-    def h_ref(t, s):
-        return hid.at[s, pl.ds(t * TH, TH)]
-
-    def h_send(t):
-        send(h_ref(t, xh), h_ref(t, xh), hs.at[t], hr.at[t], dev(xh_=1 - xh))
-
-    def rotate(t):
-        if t == 0:
+    def h_ref(q, s):
+        return hid.at[s, pl.ds(q * HX, HX)]
+
+    def h_send(q):
+        send(h_ref(q, xh), h_ref(q, xh), hs.at[q], hr.at[q], dev(xh_=1 - xh))
+
+    def rotate(q):
+        if not rotated:
             loads[4].wait()
-        recv(h_ref(t, 1 - xh), hs.at[t], hr.at[t], dev(xh_=1 - xh))
-        rows = pl.ds(t * TH, TH)
+        rotated.add(q)
+        for i in range(q * TQ // HX, (q + 1) * TQ // HX):
+            recv(h_ref(i, 1 - xh), hs.at[i], hr.at[i], dev(xh_=1 - xh))
+        rows = pl.ds(q * TQ, TQ)
         for n0, n in ((0, 256), (256, 256), (512, 256), (768, 128)):
             m = hbuf[:, n0:n0 + n]
             l0 = jnp.dot(hid[0, rows], m, preferred_element_type=F32)
@@ -257,120 +276,214 @@
             rot[rows, n0:n0 + n] = ((l0 + l1) * scale).astype(BF)
             rot[rows, KL + n0:KL + n0 + n] = ((l0 - l1) * scale).astype(BF)
 
-    def partial(p, j, t, g):
+    rotated = set()
+    complete = set()
+
+    def partial(j, q, g):
+        if (j, g) not in complete:
+            w_wait(j, g)
+            complete.add((j, g))
         first, n = GROUPS[g]
         for i in range(0, n, 2):
             w = min(2, n - i) * CW
             c0 = (first + i) * CW
-            part[p % 2, :, c0:c0 + w] = jnp.dot(
-                rot[pl.ds(t * TH, TH)], wbuf[j, :, c0:c0 + w], preferred_element_type=F32)
-
-    def own_part(p, half, m):
+            part[j, pl.ds(q * TQ, TQ), c0:c0 + w] = jnp.dot(
+                rot[pl.ds(q * TQ, TQ)], wbuf[j, :, c0:c0 + w], preferred_element_type=F32)
+
+    def own_part(j, q, m):
         c0 = place(m) * CW
-        return part[p % 2, half * TQ:(half + 1) * TQ, c0:c0 + CW]
-
-    def rs_wait(p, k, m):
-        _, half, d, _ = CHAINS[k]
-        recv(rrecv.at[p, k, m], rs.at[p, k, m], rr.at[p, k, m], dev(z_=zat(-d)))
+        return part[j, pl.ds(q * TQ, TQ), c0:c0 + CW]
+
+    def rs_wait(j, q, k, m):
+        p = j * NQ + q
+        recv(rrecv.at[p, k, m], rs.at[p, k, m], rr.at[p, k, m], dev(z_=zat(-chain(q, k)[0])))
         return rrecv[p, k, m].astype(F32)
 
-    def rs_hop(p, k, m):
-        _, half, d, first = CHAINS[k]
-        value = own_part(p, half, d * m)
+    def rs_hop(j, q, k, m):
+        p = j * NQ + q
+        d, first = chain(q, k)
+        value = own_part(j, q, d * m)
         if m < first:
-            value = value + rs_wait(p, k, m)
+            value = value + rs_wait(j, q, k, m)
         rsend[p, k, m - 1] = value.astype(BF)
         send(rsend.at[p, k, m - 1], rrecv.at[p, k, m - 1], rs.at[p, k, m - 1], rr.at[p, k, m - 1],
              dev(z_=zat(d)))
 
-    def rs_step(p, s):
-        for k in range(4):
-            m = CHAINS[k][3] - s
-            if m >= 1:
-                rs_hop(p, k, m)
-
-    def rs_final(p, j, t):
-        for half, (ka, kb) in ((0, (3, 0)), (1, (2, 1))):
-            value = own_part(p, half, 0) + rs_wait(p, ka, 0) + rs_wait(p, kb, 0)
-            c0 = t * TH + half * TQ
-            out[j * CW:(j + 1) * CW, c0:c0 + TQ] = value.T.astype(BF)
-
+    def rs_final(j, q):
+        value = own_part(j, q, 0) + rs_wait(j, q, 0, 0) + rs_wait(j, q, 1, 0)
+        out[j * CW:(j + 1) * CW, q * TQ:(q + 1) * TQ] = value.T.astype(BF)
+
+    load_all()
+    silu(0)
+    silu(1)
+    meet()
     p1_send(0)
     p1_send(1)
-    silu(0)
     h_send(0)
+    h_send(1)
+    h_send(2)
+    h_send(3)
     p1_wait_rotate(0)
     p2_send(0)
-    silu(1)
+    h_send(4)
+    h_send(5)
     p1_wait_rotate(1)
     p2_send(1)
-    p2_wait(0)
-    for g in range(NG):
-        x_send(0, g)
-    h_send(1)
-    for g in range(NG):
-        y_own(0, g)
-    y_near(0, 0)
-    p2_wait(1)
-    for g in range(NG):
-        x_send(1, g)
+    x_send(0, 0)
+    h_send(6)
+    rotate(0)
+    x_send(0, 1)
+    h_send(7)
+    x_send(0, 2)
+    x_send(0, 3)
+    h_send(8)
+    x_send(1, 0)
+    y_own(0, 0)
+    x_send(1, 1)
+    h_send(9)
+    x_send(1, 2)
+    y_near(0, 0, 0)
+    y_near(0, 0, 1)
+    y_own(0, 1)
+    x_send(1, 3)
+    h_send(10)
     y_far(0, 0)
-    y_near(0, 1)
-    rotate(0)
-    c_wait(0, 0)
-    partial(0, 0, 0, 0)
-    rs_step(0, 0)
+    rotate(1)
+    y_own(0, 2)
+    partial(0, 0, 0)
+    rs_hop(0, 0, 0, 4)
+    y_near(0, 1, 0)
+    y_near(0, 1, 1)
+    partial(0, 1, 0)
+    rs_hop(0, 1, 1, 4)
+    y_own(0, 3)
+    h_send(11)
+    y_own(1, 0)
+    y_near(0, 2, 0)
+    y_near(0, 2, 1)
+    y_own(1, 1)
     y_far(0, 1)
-    y_near(0, 2)
-    for g in range(NG):
-        y_own(1, g)
-    c_wait(0, 1)
-    partial(0, 0, 0, 1)
-    rs_step(0, 1)
+    partial(0, 0, 1)
+    rs_hop(0, 0, 0, 3)
+    rs_hop(0, 0, 1, 3)
+    partial(0, 1, 1)
+    h_send(12)
+    rs_hop(0, 1, 0, 3)
+    rs_hop(0, 1, 1, 3)
+    y_own(1, 2)
+    y_near(0, 3, 0)
+    y_near(0, 3, 1)
+    y_near(1, 0, 0)
+    y_near(1, 0, 1)
+    y_own(1, 3)
     y_far(0, 2)
-    c_wait(0, 2)
-    partial(0, 0, 0, 2)
-    rs_step(0, 2)
-    y_near(1, 0)
-    rs_step(0, 3)
+    partial(0, 0, 2)
+    rs_hop(0, 0, 0, 2)
+    h_send(13)
+    rs_hop(0, 0, 1, 2)
+    partial(0, 1, 2)
+    y_near(1, 1, 0)
+    y_near(1, 1, 1)
+    rs_hop(0, 1, 0, 2)
+    rs_hop(0, 1, 1, 2)
+    h_send(14)
+    rotate(2)
+    y_near(1, 2, 0)
+    y_near(1, 2, 1)
+    partial(0, 2, 0)
+    rs_hop(0, 2, 0, 4)
+    partial(0, 2, 1)
+    y_far(0, 3)
+    h_send(15)
+    rs_hop(0, 2, 1, 3)
     y_far(1, 0)
-    rotate(1)
-    for g in range(NG):
-        partial(1, 0, 1, g)
-    rs_step(1, 0)
-    y_near(1, 1)
-    rs_final(0, 0, 0)
-    rs_step(1, 1)
+    partial(0, 2, 2)
+    partial(0, 0, 3)
+    rs_hop(0, 0, 0, 1)
+    rs_hop(0, 0, 1, 1)
+    partial(0, 1, 3)
+    rs_hop(0, 1, 0, 1)
+    rs_hop(0, 1, 1, 1)
+    rs_hop(0, 2, 0, 3)
+    partial(0, 2, 3)
+    rs_hop(0, 2, 1, 2)
+    y_near(1, 3, 0)
+    y_near(1, 3, 1)
+    partial(1, 0, 0)
+    rs_hop(1, 0, 0, 4)
+    partial(1, 1, 0)
+    rs_hop(1, 1, 1, 4)
     y_far(1, 1)
-    y_near(1, 2)
-    c_wait(1, 0)
-    partial(2, 1, 0, 0)
-    rs_step(2, 0)
-    rs_step(1, 2)
+    partial(1, 2, 0)
+    rs_hop(1, 2, 0, 4)
+    rs_final(0, 0)
     y_far(1, 2)
-    c_wait(1, 1)
-    partial(2, 1, 0, 1)
-    rs_step(1, 3)
-    rs_step(2, 1)
-    c_wait(1, 2)
-    partial(2, 1, 0, 2)
-    rs_final(1, 0, 1)
-    rs_step(2, 2)
-    for g in range(NG):
-        partial(3, 1, 1, g)
-    rs_step(3, 0)
-    rs_step(2, 3)
-    rs_step(3, 1)
-    rs_final(2, 1, 0)
-    rs_step(3, 2)
-    rs_step(3, 3)
-    rs_final(3, 1, 1)
+    partial(1, 0, 1)
+    rs_hop(1, 0, 1, 3)
+    partial(1, 1, 1)
+    rs_hop(1, 1, 0, 3)
+    partial(1, 0, 2)
+    rs_hop(0, 2, 0, 2)
+    y_far(1, 3)
+    rs_hop(0, 2, 1, 1)
+    partial(1, 1, 2)
+    partial(1, 2, 1)
+    rs_hop(1, 0, 0, 3)
+    rs_hop(1, 1, 1, 3)
+    rs_hop(1, 2, 1, 3)
+    partial(1, 0, 3)
+    partial(1, 1, 3)
+    rs_hop(1, 0, 1, 2)
+    rs_hop(1, 2, 0, 3)
+    partial(1, 2, 2)
+    partial(1, 2, 3)
+    rs_hop(1, 1, 0, 2)
+    rotate(3)
+    rs_hop(0, 2, 0, 1)
+    rs_hop(1, 1, 1, 2)
+    partial(0, 3, 0)
+    rs_hop(0, 3, 1, 4)
+    partial(0, 3, 1)
+    rs_hop(1, 0, 0, 2)
+    rs_hop(0, 3, 0, 3)
+    rs_hop(1, 2, 1, 2)
+    partial(0, 3, 2)
+    partial(0, 3, 3)
+    rs_hop(1, 0, 1, 1)
+    rs_hop(1, 2, 0, 2)
+    partial(1, 3, 0)
+    rs_hop(1, 3, 1, 4)
+    partial(1, 3, 1)
+    rs_hop(1, 1, 0, 1)
+    rs_hop(1, 1, 1, 1)
+    rs_hop(1, 3, 0, 3)
+    partial(1, 3, 2)
+    partial(1, 3, 3)
+    rs_hop(0, 3, 1, 3)
+    rs_final(0, 1)
+    rs_final(0, 2)
+    rs_hop(1, 0, 0, 1)
+    rs_hop(1, 2, 1, 1)
+    rs_hop(0, 3, 0, 2)
+    rs_hop(1, 2, 0, 1)
+    rs_hop(1, 3, 1, 3)
+    rs_final(1, 1)
+    rs_hop(1, 3, 0, 2)
+    rs_hop(0, 3, 1, 2)
+    rs_final(1, 0)
+    rs_hop(0, 3, 0, 1)
+    rs_hop(1, 3, 1, 2)
+    rs_final(1, 2)
+    rs_hop(0, 3, 1, 1)
+    rs_hop(1, 3, 0, 1)
+    rs_hop(1, 3, 1, 1)
+    rs_final(0, 3)
+    rs_final(1, 3)
 
     for c in sent:
         c.wait_send()
-    for j in range(2):
-        for g in range(NG):
-            x_finish(j, g)
+    for j, g in crossing:
+        x_finish(j, g)
 
 
 def body(gate_pre, up_pre, down_weight):
@@ -392,21 +505,21 @@
             pltpu.VMEM((2, NZ, KB, CW), BF),
             pltpu.VMEM((2, KB, NZ * CW), BF),
             pltpu.VMEM((2, 2 * KL, NZ * CW), BF),
-            pltpu.VMEM((2, TH, NZ * CW), F32),
-            pltpu.VMEM((4, 4, 4, TQ, CW), BF),
-            pltpu.VMEM((4, 4, 4, TQ, CW), BF),
+            pltpu.VMEM((2, TOKENS, NZ * CW), F32),
+            pltpu.VMEM((2 * NQ, 2, 4, TQ, CW), BF),
+            pltpu.VMEM((2 * NQ, 2, 4, TQ, CW), BF),
             dma((5,)),
             dma((2, NZ)), dma((2, NZ)),
             dma((2, NZ)), dma((2, NZ)),
             dma((2, NG, 2)), dma((2, NG, 2)),
             dma((2, NG, 4)), dma((2, NG, 4)),
             dma((2, NG, 4)), dma((2, NG, 4)),
-            dma((2,)), dma((2,)),
-            dma((4, 4, 4)), dma((4, 4, 4)),
+            dma((TOKENS // HX,)), dma((TOKENS // HX,)),
+            dma((2 * NQ, 2, 4)), dma((2 * NQ, 2, 4)),
         ],
         compiler_params=pltpu.CompilerParams(
             collective_id=0, has_side_effects=True, vmem_limit_bytes=56 << 20),
-        name="rotated_down_projection",
+        name=NAME,
     )(gate_pre.reshape(KL, TOKENS), up_pre.reshape(KL, TOKENS),
       down_weight.reshape(KL, 16 * 2 * CW), hmat)
 

time: 126 us -> 103 us (0.82)
  Pallas kernels: 123 us -> 100 us
    pallas_call x1, Pallas kernels: 123 us -> 100 us  [body(): pl.pallas_call(functools.partial(kernel, 1.0 / math.sqrt(16 * KL)), out_s...]
where the time goes in v2:
time: 103 us; the launch traced here: 102 us
  Pallas kernels  100 us (97%)
  local copies, waits for them, and re-layouts  1.87 us (2%)
    pallas_call x1, Pallas kernels, body(): pl.pallas_call(functools.partial(kernel, 1.0 / math.sqrt(16 * KL)), out_s...  100 us

profile of v2, /device:TPU:32, one launch (start us, length us, event | category | flops | bytes accessed | tf_op | source)
XLA Modules:
  0.0 102.1 jit_solution(13110665538451659414)
XLA Ops:
  0.0 100.2 %rotated_down_projection.1 = bf16[256,1024]{1,0:T(8,128)(2,1)} custom-call(bf16[896,1024]{1,0:T(8,128)(2,1)} %bitcast.4, bf16[896,1024]{1,0:T(8,128)(2,1)} %bitcast.5, bf16[896,4096]{1,0:T(8,128)(2,1)} %bitcast.3, bf16[896,896]{1,0:T(8,128)(2,1)} %constant.2.clone.hmat), custom_call_target="tpu_custom_call" | custom-call | tf_op jit(solution)/shard_map/rotated_down_projection/pallas_call | solution.py:493
  100.2 1.9 %copy.6 = bf16[256,1024]{1,0:T(8,128)(2,1)} copy(bf16[256,1024]{1,0:T(8,128)(2,1)} %rotated_down_projection.1) | data formatting | bytes 1048576

commit v3 on v2

--- a/solution.py
+++ b/solution.py
@@ -315,13 +315,13 @@
 
     load_all()
     silu(0)
-    silu(1)
     meet()
     p1_send(0)
     p1_send(1)
     h_send(0)
     h_send(1)
     h_send(2)
+    silu(1)
     h_send(3)
     p1_wait_rotate(0)
     p2_send(0)

time: 103 us -> 102 us (level)
  no operation moved by 1% of the time
where the time goes in v3:
time: 102 us
  Pallas kernels  100 us (98%)
  local copies, waits for them, and re-layouts  1.87 us (2%)
    pallas_call x1, Pallas kernels, body(): pl.pallas_call(functools.partial(kernel, 1.0 / math.sqrt(16 * KL)), out_s...  100 us

profile of v3, /device:TPU:32, one launch (start us, length us, event | category | flops | bytes accessed | tf_op | source)
XLA Modules:
  0.0 102.0 jit_solution(8253461582536574737)
XLA Ops:
  0.0 100.1 %rotated_down_projection.1 = bf16[256,1024]{1,0:T(8,128)(2,1)} custom-call(bf16[896,1024]{1,0:T(8,128)(2,1)} %bitcast.4, bf16[896,1024]{1,0:T(8,128)(2,1)} %bitcast.5, bf16[896,4096]{1,0:T(8,128)(2,1)} %bitcast.3, bf16[896,896]{1,0:T(8,128)(2,1)} %constant.2.clone.hmat), custom_call_target="tpu_custom_call" | custom-call | tf_op jit(solution)/shard_map/rotated_down_projection/pallas_call | solution.py:493
  100.1 1.9 %copy.6 = bf16[256,1024]{1,0:T(8,128)(2,1)} copy(bf16[256,1024]{1,0:T(8,128)(2,1)} %rotated_down_projection.1) | data formatting | bytes 1048576

commit v4 on v3

--- a/solution.py
+++ b/solution.py
@@ -311,7 +311,7 @@
 
     def rs_final(j, q):
         value = own_part(j, q, 0) + rs_wait(j, q, 0, 0) + rs_wait(j, q, 1, 0)
-        out[j * CW:(j + 1) * CW, q * TQ:(q + 1) * TQ] = value.T.astype(BF)
+        out[q * TQ:(q + 1) * TQ, j * CW:(j + 1) * CW] = value.astype(BF)
 
     load_all()
     silu(0)
@@ -492,7 +492,7 @@
     any_spec = pl.BlockSpec(memory_space=pl.ANY)
     return pl.pallas_call(
         functools.partial(kernel, 1.0 / math.sqrt(16 * KL)),
-        out_shape=jax.ShapeDtypeStruct((2 * CW, TOKENS), BF),
+        out_shape=jax.ShapeDtypeStruct((TOKENS, 2 * CW), BF),
         in_specs=[any_spec] * 4,
         out_specs=pl.BlockSpec(memory_space=pltpu.VMEM),
         scratch_shapes=[
@@ -521,7 +521,7 @@
             collective_id=0, has_side_effects=True, vmem_limit_bytes=56 << 20),
         name=NAME,
     )(gate_pre.reshape(KL, TOKENS), up_pre.reshape(KL, TOKENS),
-      down_weight.reshape(KL, 16 * 2 * CW), hmat)
+      down_weight.reshape(KL, 16 * 2 * CW), hmat).T
 
 
 def solution(mesh):

time: 102 us -> 102 us (level)
    transpose x0 -> x1, local copies, waits for them, and re-layouts: none -> 2.04 us  [body(): return pl.pallas_call(functools.partial(kernel, 1.0 / math.sqrt(16 * KL))...]
    unnamed x1 -> x0, local copies, waits for them, and re-layouts: 1.87 us -> none
where the time goes in v4:
time: 102 us
  Pallas kernels  100 us (98%)
  local copies, waits for them, and re-layouts  2.04 us (2%)
    pallas_call x1, Pallas kernels, body(): pl.pallas_call(functools.partial(kernel, 1.0 / math.sqrt(16 * KL)), out_s...  100 us
    transpose x1, local copies, waits for them, and re-layouts, body(): return pl.pallas_call(functools.partial(kernel, 1.0 / math.sqrt(16 * KL))...  2.04 us

profile of v4, /device:TPU:32, one launch (start us, length us, event | category | flops | bytes accessed | tf_op | source)
XLA Modules:
  0.0 102.2 jit_solution(15658579741175322656)
XLA Ops:
  0.0 100.1 %rotated_down_projection.1 = bf16[1024,256]{1,0:T(8,128)(2,1)} custom-call(bf16[896,1024]{1,0:T(8,128)(2,1)} %bitcast.6, bf16[896,1024]{1,0:T(8,128)(2,1)} %bitcast.7, bf16[896,4096]{1,0:T(8,128)(2,1)} %bitcast.4, bf16[896,896]{1,0:T(8,128)(2,1)} %constant.2.clone.hmat), custom_call_target="tpu_custom_call" | custom-call | tf_op jit(solution)/shard_map/rotated_down_projection/pallas_call | solution.py:493
  100.1 2.0 %copy.5 = bf16[256,1024]{1,0:T(8,128)(2,1)} copy(bf16[256,1024]{0,1:T(8,128)(2,1)} %bitcast.5) | data formatting | bytes 1048576 | tf_op jit(solution)/shard_map/transpose | solution.py:524
